TPU v7x, 32 devices: a whole 2x2x4 slice. The times are simulated.
32 devices in a mesh: scan: 8 (over z, x), bin: 4 (over y, core).
Axes of the slice: x: 2, y: 2, z: 4, core: 2. Of those that a mesh axis runs over, the one named last changes fastest.
Arguments:
- tile_blocks: bfloat16 [64, 16, 256, 256], P('scan', 'bin'), may hold values from -0.25 to 0.25
- tile_pattern: int32 [2, 64], P(None, 'scan'), may hold values from 0 to 63, as said below
- tile_count: int32 [8], P('scan'), may hold values from 1 to 8, as said below
- initial_map: float32 [16, 4, 4096], P('bin', None, 'scan')
- measured: float32 [16, 4, 16384], P('bin', None, 'scan')
- step_size: float32 [1], replicated, may hold values from 0.06 to 0.1
- penalty: float32 [4096], P('scan'), may hold values from 40 to 200
Outputs:
- source_map: float32 [16, 4, 4096], P('bin', None, 'scan')
Inputs may be any that keep to these rules, and one draw needn't show every extreme that they name: `tile_pattern`: row 0 names a sensor block of 64; row 1 of slot s names one of the 2 scan tiles (s // 8) * 2 to (s // 8) * 2 + 1. Only the first tile_count[d] slots of index d of scan are live; in every draw some indices have all 8 slots live.
All inputs are finite; a program needn't handle non-finite values.
Results may differ from a plain program's by a relative error of at most 0.00074.
Values may be sent and summed in bfloat16 or wider, within the bound.
No kernel may reach another device: no remote copies, remote signals or barrier semaphores. Data moves between devices by JAX's collectives and lax.ppermute only.
A program may use at most 64 MiB of HBM per device.

v0:
```python
import jax
import jax.numpy as jnp
from jax import lax
from jax.sharding import PartitionSpec as P

ITERS = 2


def add_forward(partial_value, tile_set, block_rows, block_cols, points, first_slot, end_slot):
    tile_width = tile_set.shape[-1]

    def advance(slot_id, running):
        matrix = lax.dynamic_index_in_dim(tile_set, slot_id, 0, keepdims=False)
        source = lax.dynamic_slice_in_dim(points, block_cols[slot_id] * tile_width, tile_width, 2)
        contrib = jnp.einsum("fij,fsj->fsi", matrix, source, preferred_element_type=jnp.float32)
        start = block_rows[slot_id] * tile_width
        present = lax.dynamic_slice_in_dim(running, start, tile_width, 2)
        return lax.dynamic_update_slice_in_dim(running, present + contrib, start, 2)

    return lax.fori_loop(first_slot, end_slot, advance, partial_value)


def add_backward(gradient, tile_set, block_rows, block_cols, residual, first_slot, end_slot):
    tile_width = tile_set.shape[-1]

    def advance(slot_id, running):
        matrix = lax.dynamic_index_in_dim(tile_set, slot_id, 0, keepdims=False)
        source = lax.dynamic_slice_in_dim(residual, block_rows[slot_id] * tile_width, tile_width, 2)
        contrib = jnp.einsum("fij,fsi->fsj", matrix, source, preferred_element_type=jnp.float32)
        start = block_cols[slot_id] * tile_width
        present = lax.dynamic_slice_in_dim(running, start, tile_width, 2)
        return lax.dynamic_update_slice_in_dim(running, present + contrib, start, 2)

    return lax.fori_loop(first_slot, end_slot, advance, gradient)


def home_slots(rows, tile_width, sensors_dev, homed):
    return rows * tile_width // sensors_dev * homed + rows % homed


def body(tile_blocks, tile_pattern, tile_count, initial_map, measured, step_size, penalty):
    tile_width = tile_blocks.shape[-1]
    per_device = initial_map.shape[2] // tile_width
    block_rows = tile_pattern[0]
    block_cols = tile_pattern[1] - lax.axis_index("scan") * per_device
    live_count = tile_count[0]
    bins_dev, snapshots, sensors_dev = measured.shape
    scan_count = lax.axis_size("scan")
    sensors = sensors_dev * scan_count
    homed = max(1, sensors_dev // tile_width)
    measured_all = lax.all_gather(measured, "scan", axis=2, tiled=True)
    block_rows = home_slots(block_rows, tile_width, sensors_dev, homed)
    own_measured = lax.dynamic_slice_in_dim(
        measured_all, lax.axis_index("scan") * sensors_dev, homed * tile_width, 2
    )
    sensors = scan_count * homed * tile_width
    current = initial_map
    for iteration in range(ITERS):
        rounded_map = current.astype(jnp.bfloat16)
        partial_value = jnp.zeros((bins_dev, snapshots, sensors), jnp.float32)
        partial_value = add_forward(
            partial_value, tile_blocks, block_rows, block_cols, rounded_map, 0, live_count
        )
        outgoing = partial_value.reshape(bins_dev, snapshots, scan_count, homed * tile_width)
        arrived = lax.all_to_all(outgoing, "scan", split_axis=2, concat_axis=2, tiled=True)
        totals = jnp.sum(arrived, axis=2)
        rounded = (totals - own_measured).astype(jnp.bfloat16)
        residual = lax.all_gather(rounded, "scan", axis=2, tiled=True)
        gradient = jnp.zeros_like(current)
        gradient = add_backward(
            gradient, tile_blocks, block_rows, block_cols, residual, 0, live_count
        )
        moved = current - step_size[0] * gradient
        energy = lax.psum(jnp.sum(moved * moved, axis=(0, 1)), "bin")
        current = moved * jnp.maximum(0.0, 1.0 - step_size[0] * penalty / jnp.sqrt(energy + 1e-06))
    return current


def solution(mesh):
    in_specs = (
        P("scan", "bin", None, None),
        P(None, "scan"),
        P("scan"),
        P("bin", None, "scan"),
        P("bin", None, "scan"),
        P(),
        P("scan"),
    )
    out_specs = P("bin", None, "scan")
    return jax.shard_map(body, mesh=mesh, in_specs=in_specs, out_specs=out_specs, check_vma=False)
```

profile of v0, /device:TPU:12, one launch (start us, length us, event | category | flops | bytes accessed | tf_op | source)
XLA Modules:
  0.0 327.0 jit_solution(14422891736312756115)
XLA Ops:
  6.5 0.7 fusion.20
  7.2 0.7 subtract_bitcast_fusion
  7.9 0.8 convert_element_type.12
  8.8 38.3 %while.40 = (s32[]{:T(128)}, f32[4,4,16384]{2,1,0:T(4,128)S(1)}, s32[]{:T(128)}, s32[8]{0:T(128)S(1)}, s32[8]{0:T(128)S(1)}, /*index=5*/bf16[4,4,512]{2,1,0:T(4,...) while((s32[]{:T(128)}, f32[4,4,16384]{2,1,0:T(4,128)S(1)}, ...), condition=%wide.region_1.2_spmd, body=%wide.region_0.1_spmd.sunk | while | flops 2101261 | bytes 565535 | solution.py:20
  10.9 0.7 dynamic_slice.118
  12.2 1.3 fusion.36
  15.6 0.7 dynamic_slice.118
  16.9 1.3 fusion.36
  20.3 0.7 dynamic_slice.118
  21.6 1.3 fusion.36
  25.0 0.7 dynamic_slice.118
  26.4 1.3 fusion.36
  29.7 0.7 dynamic_slice.118
  31.1 1.3 fusion.36
  34.4 0.7 dynamic_slice.118
  35.8 1.3 fusion.36
  39.1 0.7 dynamic_slice.118
  40.5 1.3 fusion.36
  43.8 0.7 dynamic_slice.118
  45.2 1.3 fusion.36
  47.2 1.1 copy.15
  48.3 5.5 %all-to-all-start = ((f32[4,4,8,2048]{3,1,0,2:T(4,128)}), f32[4,4,8,2048]{3,1,0,2:T(4,128)S(1)}, u32[]{:S(2)}, u32[]{:S(2)}) async-start(f32[4,4,8,2048]{3,1,0,2:T(4,128)} %bitcast.36), calls=%async_computation | async-start | bytes 2097152 | tf_op jit(solution)/shard_map/all_to_all | solution.py:65
  53.7 0.7 all-gather.2.cloned.1.call-update
  55.1 26.2 %all-to-all-done = f32[4,4,8,2048]{3,1,0,2:T(4,128)S(1)} async-done(((f32[4,4,8,2048]{3,1,0,2:T(4,128)}), f32[4,4,8,2048]{3,1,0,2:T(4,128)S(1)}, u32[]{:S(2)}, u32[]{:S(2)}) %all-to-all-start) | async-done | bytes 1048608 | tf_op jit(solution)/shard_map/all_to_all | solution.py:65
  81.5 20.1 %all-gather.2.cloned.1.call-done = f32[4,4,16384]{2,1,0:T(4,128)} async-done(((f32[4,4,2048]{2,1,0:T(4,128)}), f32[4,4,16384]{2,1,0:T(4,128)}) %all-gather.2.cloned.1.call-update) | async-done | bytes 1048592 | tf_op jit(solution)/shard_map/all_gather | solution.py:51
  101.6 0.9 subtract_convert_fusion.1
  102.6 29.9 %all_gather.10 = bf16[4,4,16384]{2,1,0:T(4,128)(2,1)S(1)} all-gather(bf16[4,4,2048]{2,1,0:T(4,128)(2,1)S(1)} %subtract_convert_fusion.1), channel_id=1, replica_groups=mesh['scan'=8,'bin'=4] {'scan'}, dimensions={2}, use_global_device_ids=true | all-gather | bytes 589824 | tf_op jit(solution)/shard_map/all_gather | solution.py:68
  132.5 37.8 %while.41 = (s32[]{:T(128)}, f32[4,4,512]{2,1,0:T(4,128)S(1)}, s32[]{:T(128)}, s32[8]{0:T(128)S(1)}, s32[8]{0:T(128)S(1)}, /*index=5*/bf16[4,4,16384]{2,1,0:T(4,...) while((s32[]{:T(128)}, f32[4,4,512]{2,1,0:T(4,128)S(1)}, ...), condition=%wide.region_4.5_spmd, body=%wide.region_3.4_spmd.sunk | while | flops 2101261 | bytes 565535 | solution.py:34
  135.9 1.2 fusion.39
  140.5 1.2 fusion.39
  145.2 1.2 fusion.39
  149.8 1.2 fusion.39
  154.5 1.2 fusion.39
  159.1 1.2 fusion.39
  163.7 1.2 fusion.39
  168.4 1.2 fusion.39
  170.3 5.9 %psum.14 = f32[512]{0:T(512)S(1)} all-reduce(f32[512]{0:T(512)S(1)} %get-tuple-element.217), channel_id=1, replica_groups=mesh['scan'=8,'bin'=4] {'bin'}, use_global_device_ids=true, to_apply=%region_6.7 | all-reduce | flops 512 | bytes 4096 | tf_op jit(solution)/shard_map/psum | solution.py:74
  176.4 38.3 %while.42 = (s32[]{:T(128)}, f32[4,4,16384]{2,1,0:T(4,128)S(1)}, s32[]{:T(128)}, s32[8]{0:T(128)S(1)}, s32[8]{0:T(128)S(1)}, /*index=5*/bf16[4,4,512]{2,1,0:T(4,...) while((s32[]{:T(128)}, f32[4,4,16384]{2,1,0:T(4,128)S(1)}, ...), condition=%wide.region_8.9_spmd, body=%wide.region_7.8_spmd.sunk | while | flops 2101261 | bytes 565535 | solution.py:20
  179.8 1.3 fusion.42
  184.5 1.3 fusion.42
  189.2 1.3 fusion.42
  193.9 1.3 fusion.42
  198.6 1.3 fusion.42
  203.3 1.3 fusion.42
  208.0 1.3 fusion.42
  212.7 1.3 fusion.42
  214.7 1.1 copy.14
  215.8 5.1 %all-to-all-start.1 = ((f32[4,4,8,2048]{3,1,0,2:T(4,128)}), f32[4,4,8,2048]{3,1,0,2:T(4,128)S(1)}, u32[]{:S(2)}, u32[]{:S(2)}) async-start(f32[4,4,8,2048]{3,1,0,2:T(4,128)} %bitcast.35), calls=%async_computation.1 | async-start | bytes 2097152 | tf_op jit(solution)/shard_map/all_to_all | solution.py:65
  220.9 23.2 %all-to-all-done.1 = f32[4,4,8,2048]{3,1,0,2:T(4,128)S(1)} async-done(((f32[4,4,8,2048]{3,1,0,2:T(4,128)}), f32[4,4,8,2048]{3,1,0,2:T(4,128)S(1)}, u32[]{:S(2)}, u32[]{:S(2)}) %all-to-all-start.1) | async-done | bytes 1048608 | tf_op jit(solution)/shard_map/all_to_all | solution.py:65
  244.3 0.9 subtract_convert_fusion
  245.2 30.7 %all_gather.11 = bf16[4,4,16384]{2,1,0:T(4,128)(2,1)S(1)} all-gather(bf16[4,4,2048]{2,1,0:T(4,128)(2,1)S(1)} %subtract_convert_fusion), channel_id=1, replica_groups=mesh['scan'=8,'bin'=4] {'scan'}, dimensions={2}, use_global_device_ids=true | all-gather | bytes 589824 | tf_op jit(solution)/shard_map/all_gather | solution.py:68
  275.9 37.8 %while.43 = (s32[]{:T(128)}, f32[4,4,512]{2,1,0:T(4,128)S(1)}, s32[]{:T(128)}, s32[8]{0:T(128)S(1)}, s32[8]{0:T(128)S(1)}, /*index=5*/bf16[4,4,16384]{2,1,0:T(4,...) while((s32[]{:T(128)}, f32[4,4,512]{2,1,0:T(4,128)S(1)}, ...), condition=%wide.region_11.12_spmd, body=%wide.region_10.11_spmd.sunk | while | flops 2101261 | bytes 565535 | solution.py:34
  278.0 0.7 dynamic_slice.133
  279.4 1.2 fusion.45
  282.6 0.7 dynamic_slice.133
  284.0 1.2 fusion.45
  287.3 0.7 dynamic_slice.133
  288.6 1.2 fusion.45
  293.3 1.2 fusion.45
  297.9 1.2 fusion.45
  302.6 1.2 fusion.45
  307.2 1.2 fusion.45
  311.9 1.2 fusion.45
  313.8 5.8 %psum.15 = f32[512]{0:T(512)S(1)} all-reduce(f32[512]{0:T(512)S(1)} %multiply_reduce_fusion), channel_id=1, replica_groups=mesh['scan'=8,'bin'=4] {'bin'}, use_global_device_ids=true, to_apply=%region_13.14 | all-reduce | flops 512 | bytes 4096 | tf_op jit(solution)/shard_map/psum | solution.py:74
  (70 shorter events, 36.7 us)
Async XLA Ops:
  48.3 122.0 %copy-start = (f32[4,4,512]{2,1,0:T(4,128)S(1)}, f32[4,4,512]{2,1,0:T(4,128)}, u32[]{:S(2)}) copy-start(f32[4,4,512]{2,1,0:T(4,128)} %param.18) | copy-start | bytes 98308
  48.3 127.9 %copy-start.1 = (f32[512]{0:T(512)S(1)}, f32[512]{0:T(512)}, u32[]{:S(2)}) copy-start(f32[512]{0:T(512)} %param.21) | copy-start | bytes 6148
  48.3 33.0 %all-to-all-start = ((f32[4,4,8,2048]{3,1,0,2:T(4,128)}), f32[4,4,8,2048]{3,1,0,2:T(4,128)S(1)}, u32[]{:S(2)}, u32[]{:S(2)}) async-start(f32[4,4,8,2048]{3,1,0,2:T(4,128)} %bitcast.36), calls=%async_computation | async-start | bytes 2097152 | tf_op jit(solution)/shard_map/all_to_all | solution.py:65
  53.7 47.9 %all-gather.2.cloned.1.call-start = ((), (), s32[]{:S(2)}) async-start(), calls=%async_computation.2 | async-start | bytes 1179648 | tf_op jit(solution)/shard_map/all_gather | solution.py:51
  215.8 28.3 %all-to-all-start.1 = ((f32[4,4,8,2048]{3,1,0,2:T(4,128)}), f32[4,4,8,2048]{3,1,0,2:T(4,128)S(1)}, u32[]{:S(2)}, u32[]{:S(2)}) async-start(f32[4,4,8,2048]{3,1,0,2:T(4,128)} %bitcast.35), calls=%async_computation.1 | async-start | bytes 2097152 | tf_op jit(solution)/shard_map/all_to_all | solution.py:65
Sparse Core Ops, SparseCore 0:
  56.7 44.8 all-gather.1
where the time goes:
time: 330 us; the launch traced here: 327 us
  blocking collectives  72.3 us (22%)
  waiting for transfers between devices  70.2 us (21%)
  loops' own time  69.3 us (21%)
  local copies, waits for them, and re-layouts  45.2 us (14%)
  matrix products  40.3 us (12%)
  between operations  14.1 us (4%)
  starting transfers between devices  10.5 us (3%)
  other arithmetic  5.18 us (2%)
    all_gather x2, blocking collectives, body(): residual = lax.all_gather(rounded, 'scan', axis=2, tiled=True)  60.6 us
    all_to_all x2, waiting for transfers between devices, body(): lax.all_to_all(outgoing, 'scan', split_axis=2, concat_axis=2, tiled=True)  49.4 us
    another operation x2, loops' own time, add_forward(): return lax.fori_loop(first_slot, end_slot, advance, partial_value)  34.7 us
    another operation x2, loops' own time, add_backward(): return lax.fori_loop(first_slot, end_slot, advance, gradient)  34.5 us
    dot_general x16, matrix products, advance(): jnp.einsum('fij,fsj->fsi', matrix, source, preferred_element_type=jnp.flo...  20.6 us
    all_gather x1, waiting for transfers between devices, body(): measured_all = lax.all_gather(measured, 'scan', axis=2, tiled=True)  20.1 us
    dot_general x16, matrix products, advance(): jnp.einsum('fij,fsi->fsj', matrix, source, preferred_element_type=jnp.flo...  19.7 us
    psum x2, blocking collectives, body(): energy = lax.psum(jnp.sum(moved * moved, axis=(0, 1)), 'bin')  11.7 us
  transfers between devices with their start and end apart: 3, of which 3 were waited for; matrix products, arithmetic and copies ran while one was open for 0% of the time, Pallas kernels for 0%

commit v1 on v0

--- a/solution.py
+++ b/solution.py
@@ -4,6 +4,23 @@
 from jax.sharding import PartitionSpec as P
 
 ITERS = 2
+
+
+def in_order(tiles, dim):
+    lengths = list(tiles.shape[1:])
+    lengths[dim] *= tiles.shape[0]
+    return jnp.moveaxis(tiles, 0, dim).reshape(lengths)
+
+
+def ring_gather(x, axis, dim):
+    size = lax.axis_size(axis)
+    upward = [(i, (i + 1) % size) for i in range(size)]
+    blocks = [x]
+    while len(blocks) < size:
+        blocks.append(lax.ppermute(blocks[-1], axis, upward))
+    mine = lax.axis_index(axis)
+    blocks = jnp.stack(blocks)[(mine - jnp.arange(size)) % size]
+    return in_order(blocks, dim)
 
 
 def add_forward(partial_value, tile_set, block_rows, block_cols, points, first_slot, end_slot):
@@ -48,7 +65,7 @@
     scan_count = lax.axis_size("scan")
     sensors = sensors_dev * scan_count
     homed = max(1, sensors_dev // tile_width)
-    measured_all = lax.all_gather(measured, "scan", axis=2, tiled=True)
+    measured_all = ring_gather(measured, "scan", 2)
     block_rows = home_slots(block_rows, tile_width, sensors_dev, homed)
     own_measured = lax.dynamic_slice_in_dim(
         measured_all, lax.axis_index("scan") * sensors_dev, homed * tile_width, 2

time: 330 us -> 325 us (0.985)
  starting transfers between devices: 10.5 us -> 32 us
  between operations: 14.1 us -> 0.84 us
  waiting for transfers between devices: 70.2 us -> 57.6 us
  blocking collectives: 72.3 us -> 79 us
  loops' own time: 69.3 us -> 65.7 us
    ppermute x0 -> x7, waiting for transfers between devices: none -> 34.4 us  [ring_gather(): blocks.append(lax.ppermute(blocks[-1], axis, upward))]
    all_to_all x2, waiting for transfers between devices: 49.4 us -> 23.2 us  [body(): lax.all_to_all(outgoing, 'scan', split_axis=2, concat_axis=2, tiled=True)]
    ppermute x0 -> x7, starting transfers between devices: none -> 21.8 us  [ring_gather(): blocks.append(lax.ppermute(blocks[-1], axis, upward))]
    all_gather x1 -> x0, waiting for transfers between devices: 20.1 us -> none  [body(): measured_all = lax.all_gather(measured, 'scan', axis=2, tiled=True)]
    all_gather x2, blocking collectives: 60.6 us -> 67.3 us  [body(): residual = lax.all_gather(rounded, 'scan', axis=2, tiled=True)]
  transfers between devices with their start and end apart: 3 -> 9, of which waited for: 3 -> 7; matrix products, arithmetic and copies ran while one was open for 0% -> 8% of each run, Pallas kernels for 0% -> 0%
where the time goes in v1:
time: 325 us; the launch traced here: 322 us
  blocking collectives  79 us (24%)
  loops' own time  65.7 us (20%)
  waiting for transfers between devices  57.6 us (18%)
  local copies, waits for them, and re-layouts  43.1 us (13%)
  matrix products  40.3 us (12%)
  starting transfers between devices  32 us (10%)
  other arithmetic  3.4 us (1%)
    all_gather x2, blocking collectives, body(): residual = lax.all_gather(rounded, 'scan', axis=2, tiled=True)  67.3 us
    ppermute x7, waiting for transfers between devices, ring_gather(): blocks.append(lax.ppermute(blocks[-1], axis, upward))  34.4 us
    another operation x2, loops' own time, add_forward(): return lax.fori_loop(first_slot, end_slot, advance, partial_value)  32.9 us
    another operation x2, loops' own time, add_backward(): return lax.fori_loop(first_slot, end_slot, advance, gradient)  32.7 us
    all_to_all x2, waiting for transfers between devices, body(): lax.all_to_all(outgoing, 'scan', split_axis=2, concat_axis=2, tiled=True)  23.2 us
    ppermute x7, starting transfers between devices, ring_gather(): blocks.append(lax.ppermute(blocks[-1], axis, upward))  21.8 us
    dot_general x16, matrix products, advance(): jnp.einsum('fij,fsj->fsi', matrix, source, preferred_element_type=jnp.flo...  20.6 us
    dot_general x16, matrix products, advance(): jnp.einsum('fij,fsi->fsj', matrix, source, preferred_element_type=jnp.flo...  19.7 us
  transfers between devices with their start and end apart: 9, of which 7 were waited for; matrix products, arithmetic and copies ran while one was open for 8% of the time, Pallas kernels for 0%

profile of v1, /device:TPU:12, one launch (start us, length us, event | category | flops | bytes accessed | tf_op | source)
XLA Modules:
  0.0 321.8 jit_solution(9401226454658368087)
XLA Ops:
  0.0 1.5 collective-permute-start
  1.5 0.7 fusion.20
  2.2 0.7 subtract_bitcast_fusion
  2.9 0.8 convert_element_type.12
  3.8 36.6 %while.40 = (s32[]{:T(128)}, f32[4,4,16384]{2,1,0:T(4,128)S(1)}, s32[]{:T(128)}, s32[8]{0:T(128)S(1)}, s32[8]{0:T(128)S(1)}, /*index=5*/bf16[4,4,512]{2,1,0:T(4,...) while((s32[]{:T(128)}, f32[4,4,16384]{2,1,0:T(4,128)S(1)}, ...), condition=%wide.region_1.2_spmd, body=%wide.region_0.1_spmd.sunk | while | flops 2101261 | bytes 565535 | solution.py:37
  7.0 1.3 fusion.38
  11.5 1.3 fusion.38
  16.0 1.3 fusion.38
  20.4 1.3 fusion.38
  24.9 1.3 fusion.38
  29.4 1.3 fusion.38
  33.9 1.3 fusion.38
  38.4 1.3 fusion.38
  40.4 1.0 copy.19
  41.4 5.3 %all-to-all-start = ((f32[4,4,8,2048]{3,1,0,2:T(4,128)}), f32[4,4,8,2048]{3,1,0,2:T(4,128)S(1)}, u32[]{:S(2)}, u32[]{:S(2)}) async-start(f32[4,4,8,2048]{3,1,0,2:T(4,128)} %bitcast.57), calls=%async_computation | async-start | bytes 2097152 | tf_op jit(solution)/shard_map/all_to_all | solution.py:82
  47.5 1.5 collective-permute-start.1
  49.0 19.0 %collective-permute-done.1 = f32[4,4,2048]{2,1,0:T(4,128)S(1)} collective-permute-done((f32[4,4,2048]{2,1,0:T(4,128)S(1)}, f32[4,4,2048]{2,1,0:T(4,128)S(1)}, u32[]{:S(2)}, u32[]{:S(2)}) %collective-permute-start.1) | collective-permute-done | bytes 131104 | tf_op jit(solution)/shard_map/ppermute | solution.py:20
  68.0 5.2 %collective-permute-start.2 = (f32[4,4,2048]{2,1,0:T(4,128)S(1)}, f32[4,4,2048]{2,1,0:T(4,128)S(1)}, u32[]{:S(2)}, u32[]{:S(2)}) collective-permute-start(f32[4,4,2048]{2,1,0:T(4,128)S(1)} %collective-permute-done.1), channel_id=1, source_target_pairs={{0,4},{4,8},{8,12},{12,16},{16,20},{20,24},{24,28},{28,0},{1,5},{5... | collective-permute-start | bytes 393224 | tf_op jit(solution)/shard_map/ppermute | solution.py:20
  73.2 2.9 collective-permute-done.2
  76.1 3.4 %collective-permute-start.3 = (f32[4,4,2048]{2,1,0:T(4,128)S(1)}, f32[4,4,2048]{2,1,0:T(4,128)S(1)}, u32[]{:S(2)}, u32[]{:S(2)}) collective-permute-start(f32[4,4,2048]{2,1,0:T(4,128)S(1)} %collective-permute-done.2), channel_id=1, source_target_pairs={{0,4},{4,8},{8,12},{12,16},{16,20},{20,24},{24,28},{28,0},{1,5},{5... | collective-permute-start | bytes 393224 | tf_op jit(solution)/shard_map/ppermute | solution.py:20
  79.5 2.5 collective-permute-done.3
  82.0 3.4 %collective-permute-start.4 = (f32[4,4,2048]{2,1,0:T(4,128)S(1)}, f32[4,4,2048]{2,1,0:T(4,128)S(1)}, u32[]{:S(2)}, u32[]{:S(2)}) collective-permute-start(f32[4,4,2048]{2,1,0:T(4,128)S(1)} %collective-permute-done.3), channel_id=1, source_target_pairs={{0,4},{4,8},{8,12},{12,16},{16,20},{20,24},{24,28},{28,0},{1,5},{5... | collective-permute-start | bytes 393224 | tf_op jit(solution)/shard_map/ppermute | solution.py:20
  85.4 2.5 collective-permute-done.4
  87.9 3.3 %collective-permute-start.5 = (f32[4,4,2048]{2,1,0:T(4,128)S(1)}, f32[4,4,2048]{2,1,0:T(4,128)S(1)}, u32[]{:S(2)}, u32[]{:S(2)}) collective-permute-start(f32[4,4,2048]{2,1,0:T(4,128)S(1)} %collective-permute-done.4), channel_id=1, source_target_pairs={{0,4},{4,8},{8,12},{12,16},{16,20},{20,24},{24,28},{28,0},{1,5},{5... | collective-permute-start | bytes 393224 | tf_op jit(solution)/shard_map/ppermute | solution.py:20
  91.2 3.1 collective-permute-done.5
  94.3 3.5 %collective-permute-start.6 = (f32[4,4,2048]{2,1,0:T(4,128)S(1)}, f32[4,4,2048]{2,1,0:T(4,128)S(1)}, u32[]{:S(2)}, u32[]{:S(2)}) collective-permute-start(f32[4,4,2048]{2,1,0:T(4,128)S(1)} %collective-permute-done.5), channel_id=1, source_target_pairs={{0,4},{4,8},{8,12},{12,16},{16,20},{20,24},{24,28},{28,0},{1,5},{5... | collective-permute-start | bytes 393224 | tf_op jit(solution)/shard_map/ppermute | solution.py:20
  97.9 4.5 %collective-permute-done.6 = f32[4,4,2048]{2,1,0:T(4,128)S(1)} collective-permute-done((f32[4,4,2048]{2,1,0:T(4,128)S(1)}, f32[4,4,2048]{2,1,0:T(4,128)S(1)}, u32[]{:S(2)}, u32[]{:S(2)}) %collective-permute-start.6) | collective-permute-done | bytes 131104 | tf_op jit(solution)/shard_map/ppermute | solution.py:20
  102.4 1.2 gather_fusion
  104.0 36.6 %all_gather.6 = bf16[4,4,16384]{2,1,0:T(4,128)(2,1)S(1)} all-gather(bf16[4,4,2048]{2,1,0:T(4,128)(2,1)S(1)} %subtract_convert_fusion.1), channel_id=1, replica_groups=mesh['scan'=8,'bin'=4] {'scan'}, dimensions={2}, use_global_device_ids=true | all-gather | bytes 589824 | tf_op jit(solution)/shard_map/all_gather | solution.py:85
  140.6 36.0 %while.41 = (s32[]{:T(128)}, f32[4,4,512]{2,1,0:T(4,128)S(1)}, s32[]{:T(128)}, s32[8]{0:T(128)S(1)}, s32[8]{0:T(128)S(1)}, /*index=5*/bf16[4,4,16384]{2,1,0:T(4,...) while((s32[]{:T(128)}, f32[4,4,512]{2,1,0:T(4,128)S(1)}, ...), condition=%wide.region_4.5_spmd, body=%wide.region_3.4_spmd.sunk | while | flops 2101261 | bytes 565535 | solution.py:51
  142.5 0.6 dynamic_slice.123
  143.8 1.2 fusion.41
  148.2 1.2 fusion.41
  152.6 1.2 fusion.41
  157.0 1.2 fusion.41
  161.5 1.2 fusion.41
  165.9 1.2 fusion.41
  170.3 1.2 fusion.41
  174.7 1.2 fusion.41
  176.7 5.9 %psum.14 = f32[512]{0:T(512)S(1)} all-reduce(f32[512]{0:T(512)S(1)} %get-tuple-element.217), channel_id=1, replica_groups=mesh['scan'=8,'bin'=4] {'bin'}, use_global_device_ids=true, to_apply=%region_6.7 | all-reduce | flops 512 | bytes 4096 | tf_op jit(solution)/shard_map/psum | solution.py:91
  182.7 36.6 %while.42 = (s32[]{:T(128)}, f32[4,4,16384]{2,1,0:T(4,128)S(1)}, s32[]{:T(128)}, s32[8]{0:T(128)S(1)}, s32[8]{0:T(128)S(1)}, /*index=5*/bf16[4,4,512]{2,1,0:T(4,...) while((s32[]{:T(128)}, f32[4,4,16384]{2,1,0:T(4,128)S(1)}, ...), condition=%wide.region_8.9_spmd, body=%wide.region_7.8_spmd.sunk | while | flops 2101261 | bytes 565535 | solution.py:37
  185.9 1.3 fusion.44
  190.4 1.3 fusion.44
  194.9 1.3 fusion.44
  199.4 1.3 fusion.44
  203.9 1.3 fusion.44
  208.4 1.3 fusion.44
  212.9 1.3 fusion.44
  217.4 1.3 fusion.44
  219.3 1.0 copy.18
  220.4 4.8 %all-to-all-start.1 = ((f32[4,4,8,2048]{3,1,0,2:T(4,128)}), f32[4,4,8,2048]{3,1,0,2:T(4,128)S(1)}, u32[]{:S(2)}, u32[]{:S(2)}) async-start(f32[4,4,8,2048]{3,1,0,2:T(4,128)} %bitcast.56), calls=%async_computation.1 | async-start | bytes 2097152 | tf_op jit(solution)/shard_map/all_to_all | solution.py:82
  225.2 23.2 %all-to-all-done.1 = f32[4,4,8,2048]{3,1,0,2:T(4,128)S(1)} async-done(((f32[4,4,8,2048]{3,1,0,2:T(4,128)}), f32[4,4,8,2048]{3,1,0,2:T(4,128)S(1)}, u32[]{:S(2)}, u32[]{:S(2)}) %all-to-all-start.1) | async-done | bytes 1048608 | tf_op jit(solution)/shard_map/all_to_all | solution.py:82
  248.6 30.7 %all_gather.7 = bf16[4,4,16384]{2,1,0:T(4,128)(2,1)S(1)} all-gather(bf16[4,4,2048]{2,1,0:T(4,128)(2,1)S(1)} %subtract_convert_fusion), channel_id=1, replica_groups=mesh['scan'=8,'bin'=4] {'scan'}, dimensions={2}, use_global_device_ids=true | all-gather | bytes 589824 | tf_op jit(solution)/shard_map/all_gather | solution.py:85
  279.3 36.0 %while.43 = (s32[]{:T(128)}, f32[4,4,512]{2,1,0:T(4,128)S(1)}, s32[]{:T(128)}, s32[8]{0:T(128)S(1)}, s32[8]{0:T(128)S(1)}, /*index=5*/bf16[4,4,16384]{2,1,0:T(4,...) while((s32[]{:T(128)}, f32[4,4,512]{2,1,0:T(4,128)S(1)}, ...), condition=%wide.region_11.12_spmd, body=%wide.region_10.11_spmd.sunk | while | flops 2101261 | bytes 565535 | solution.py:51
  282.5 1.2 fusion.47
  286.9 1.2 fusion.47
  291.4 1.2 fusion.47
  295.8 1.2 fusion.47
  300.2 1.2 fusion.47
  304.6 1.2 fusion.47
  309.1 1.2 fusion.47
  313.5 1.2 fusion.47
  315.4 5.8 %psum.15 = f32[512]{0:T(512)S(1)} all-reduce(f32[512]{0:T(512)S(1)} %multiply_reduce_fusion), channel_id=1, replica_groups=mesh['scan'=8,'bin'=4] {'bin'}, use_global_device_ids=true, to_apply=%region_13.14 | all-reduce | flops 512 | bytes 4096 | tf_op jit(solution)/shard_map/psum | solution.py:91
  321.2 0.6 broadcast_multiply_fusion
  (95 shorter events, 39.9 us)
Async XLA Ops:
  0.0 47.5 %collective-permute-start = (f32[4,4,2048]{2,1,0:T(4,128)}, f32[4,4,2048]{2,1,0:T(4,128)S(1)}, u32[]{:S(2)}, u32[]{:S(2)}) collective-permute-start(f32[4,4,2048]{2,1,0:T(4,128)} %param.19), channel_id=1, source_target_pairs={{0,4},{4,8},{8,12},{12,16},{16,20},{20,24},{24,28},{28,0},{1,5},{5... | collective-permute-start | bytes 393224 | tf_op jit(solution)/shard_map/ppermute | solution.py:20
  3.6 43.1 %copy-start.1 = (f32[4,4,2048]{2,1,0:T(4,128)S(1)}, f32[4,4,2048]{2,1,0:T(4,128)}, u32[]{:S(2)}) copy-start(f32[4,4,2048]{2,1,0:T(4,128)} %param.19) | copy-start | bytes 393220
  41.4 62.3 %all-to-all-start = ((f32[4,4,8,2048]{3,1,0,2:T(4,128)}), f32[4,4,8,2048]{3,1,0,2:T(4,128)S(1)}, u32[]{:S(2)}, u32[]{:S(2)}) async-start(f32[4,4,8,2048]{3,1,0,2:T(4,128)} %bitcast.57), calls=%async_computation | async-start | bytes 2097152 | tf_op jit(solution)/shard_map/all_to_all | solution.py:82
  47.5 20.5 %collective-permute-start.1 = (f32[4,4,2048]{2,1,0:T(4,128)S(1)}, f32[4,4,2048]{2,1,0:T(4,128)S(1)}, u32[]{:S(2)}, u32[]{:S(2)}) collective-permute-start(f32[4,4,2048]{2,1,0:T(4,128)S(1)} %collective-permute-done), channel_id=1, source_target_pairs={{0,4},{4,8},{8,12},{12,16},{16,20},{20,24},{24,28},{28,0},{1,5},{5... | collective-permute-start | bytes 393224 | tf_op jit(solution)/shard_map/ppermute | solution.py:20
  68.0 8.1 %collective-permute-start.2 = (f32[4,4,2048]{2,1,0:T(4,128)S(1)}, f32[4,4,2048]{2,1,0:T(4,128)S(1)}, u32[]{:S(2)}, u32[]{:S(2)}) collective-permute-start(f32[4,4,2048]{2,1,0:T(4,128)S(1)} %collective-permute-done.1), channel_id=1, source_target_pairs={{0,4},{4,8},{8,12},{12,16},{16,20},{20,24},{24,28},{28,0},{1,5},{5... | collective-permute-start | bytes 393224 | tf_op jit(solution)/shard_map/ppermute | solution.py:20
  76.1 5.9 %collective-permute-start.3 = (f32[4,4,2048]{2,1,0:T(4,128)S(1)}, f32[4,4,2048]{2,1,0:T(4,128)S(1)}, u32[]{:S(2)}, u32[]{:S(2)}) collective-permute-start(f32[4,4,2048]{2,1,0:T(4,128)S(1)} %collective-permute-done.2), channel_id=1, source_target_pairs={{0,4},{4,8},{8,12},{12,16},{16,20},{20,24},{24,28},{28,0},{1,5},{5... | collective-permute-start | bytes 393224 | tf_op jit(solution)/shard_map/ppermute | solution.py:20
  82.0 5.9 %collective-permute-start.4 = (f32[4,4,2048]{2,1,0:T(4,128)S(1)}, f32[4,4,2048]{2,1,0:T(4,128)S(1)}, u32[]{:S(2)}, u32[]{:S(2)}) collective-permute-start(f32[4,4,2048]{2,1,0:T(4,128)S(1)} %collective-permute-done.3), channel_id=1, source_target_pairs={{0,4},{4,8},{8,12},{12,16},{16,20},{20,24},{24,28},{28,0},{1,5},{5... | collective-permute-start | bytes 393224 | tf_op jit(solution)/shard_map/ppermute | solution.py:20
  87.9 6.4 %collective-permute-start.5 = (f32[4,4,2048]{2,1,0:T(4,128)S(1)}, f32[4,4,2048]{2,1,0:T(4,128)S(1)}, u32[]{:S(2)}, u32[]{:S(2)}) collective-permute-start(f32[4,4,2048]{2,1,0:T(4,128)S(1)} %collective-permute-done.4), channel_id=1, source_target_pairs={{0,4},{4,8},{8,12},{12,16},{16,20},{20,24},{24,28},{28,0},{1,5},{5... | collective-permute-start | bytes 393224 | tf_op jit(solution)/shard_map/ppermute | solution.py:20
  94.3 8.0 %collective-permute-start.6 = (f32[4,4,2048]{2,1,0:T(4,128)S(1)}, f32[4,4,2048]{2,1,0:T(4,128)S(1)}, u32[]{:S(2)}, u32[]{:S(2)}) collective-permute-start(f32[4,4,2048]{2,1,0:T(4,128)S(1)} %collective-permute-done.5), channel_id=1, source_target_pairs={{0,4},{4,8},{8,12},{12,16},{16,20},{20,24},{24,28},{28,0},{1,5},{5... | collective-permute-start | bytes 393224 | tf_op jit(solution)/shard_map/ppermute | solution.py:20
  103.5 73.1 %copy-start = (f32[4,4,512]{2,1,0:T(4,128)S(1)}, f32[4,4,512]{2,1,0:T(4,128)}, u32[]{:S(2)}) copy-start(f32[4,4,512]{2,1,0:T(4,128)} %param.18) | copy-start | bytes 98308
  103.6 79.0 %copy-start.2 = (f32[512]{0:T(512)S(1)}, f32[512]{0:T(512)}, u32[]{:S(2)}) copy-start(f32[512]{0:T(512)} %param.21) | copy-start | bytes 6148
  220.4 28.0 %all-to-all-start.1 = ((f32[4,4,8,2048]{3,1,0,2:T(4,128)}), f32[4,4,8,2048]{3,1,0,2:T(4,128)S(1)}, u32[]{:S(2)}, u32[]{:S(2)}) async-start(f32[4,4,8,2048]{3,1,0,2:T(4,128)} %bitcast.56), calls=%async_computation.1 | async-start | bytes 2097152 | tf_op jit(solution)/shard_map/all_to_all | solution.py:82
